TPU v7x, 256 devices: a whole 4x4x8 slice. The times are simulated.
256 devices in a mesh: chan: 64 (over x, y_hi, z), band: 4 (over y_lo, core).
Axes of the slice: x: 4, y: 4 (y_hi: 2, y_lo: 2; y = y_hi * 2 + y_lo), z: 8, core: 2. Of those that a mesh axis runs over, the one named last changes fastest.
Arguments:
- spectra: float32 [2, 32, 96, 8192], P(None, None, 'band', 'chan'), may hold values from -6 to 6
- taps: float32 [96, 16], replicated, may hold values from -2.5 to 2.5
Outputs:
- stacked: bfloat16 [8, 2, 8192, 8192], P('band', None, 'chan')
All inputs are finite; a program needn't handle non-finite values.
Results may differ from a plain program's by a relative error of at most 0.0057.
Values may be sent and summed in bfloat16 or wider, within the bound.
No kernel may reach another device: no remote copies, remote signals or barrier semaphores. Data moves between devices by JAX's collectives and lax.ppermute only.
A program may use at most 192 MiB of HBM per device.

v0:
```python
import jax
import jax.numpy as jnp
from jax import lax
from jax.sharding import PartitionSpec as P

TAPS = 16
SMOOTH = 5
BAND_BINS = 12
water_level = 0.1


def padded(shard, sides, width, wrap):
    for axis, dim in sides:
        devices, length = (lax.axis_size(axis), shard.shape[dim])
        up = [(i, (i + 1) % devices) for i in range(devices if wrap else devices - 1)]
        down = [(j, i) for i, j in up]
        last = lax.slice_in_dim(shard, length - width, length, axis=dim)
        first = lax.slice_in_dim(shard, 0, width, axis=dim)
        before = lax.ppermute(last, axis, up)
        after = lax.ppermute(first, axis, down)
        shard = jnp.concatenate([before, shard, after], axis=dim)
    return shard


def fan_filter(extended, coeffs, width):
    result = jnp.zeros(extended.shape[:-1] + (width,), jnp.float32)
    for tap_index in range(coeffs.shape[1]):
        result = (
            result + coeffs[:, tap_index][:, None] * extended[..., tap_index : tap_index + width]
        )
    return result


def whiten(filtered, amp_ext, local_bins):
    smoothed = jnp.zeros(filtered.shape[1:], jnp.float32)
    for offset in range(SMOOTH):
        smoothed = smoothed + amp_ext[:, offset : offset + local_bins, :]
    smoothed = smoothed / SMOOTH
    return (filtered / (smoothed + water_level)[None]).astype(jnp.bfloat16)


def arrange(whitened, band_count):
    shaped = whitened.reshape(2, whitened.shape[1], band_count, BAND_BINS, whitened.shape[3])
    shaped = shaped.transpose(2, 0, 1, 3, 4)
    return shaped.reshape(band_count, 2 * whitened.shape[1] * BAND_BINS, whitened.shape[3])


def partner(whitened):
    return jnp.concatenate([-whitened[1:2], whitened[0:1]], axis=0)


def body(spectra, taps):
    half_taps = TAPS // 2
    reach = SMOOTH // 2
    local_bins = spectra.shape[2]
    local_chan = spectra.shape[3]
    anchor = lax.axis_index("band") * local_bins
    padded_taps = jnp.pad(taps, ((reach, reach), (0, 0)))
    coeffs = lax.dynamic_slice_in_dim(padded_taps, anchor + reach, local_bins, 0)
    extended = padded(spectra, (("chan", 3),), half_taps, True)
    filtered = fan_filter(extended, coeffs, local_chan)
    amplitude = jnp.sqrt(filtered[0] * filtered[0] + filtered[1] * filtered[1])
    amp_ext = padded(amplitude, (("band", 1),), reach, False)
    whitened = whiten(filtered, amp_ext, local_bins)
    band_count = local_bins // BAND_BINS
    features = arrange(whitened, band_count)
    scale_factor = 1.0 / (whitened.shape[1] * BAND_BINS)
    remote = lax.all_gather(whitened, "chan", axis=3, tiled=True)
    right = arrange(remote, band_count)
    turned = arrange(partner(remote), band_count)
    real_part = jnp.einsum("bki,bkj->bij", features, right, preferred_element_type=jnp.float32)
    imag_part = jnp.einsum("bki,bkj->bij", features, turned, preferred_element_type=jnp.float32)
    return (jnp.stack([real_part, imag_part], axis=1) * scale_factor).astype(jnp.bfloat16)


def solution(mesh):
    placed = (P(None, None, "band", "chan"), P())
    return jax.shard_map(
        body, mesh=mesh, in_specs=placed, out_specs=P("band", None, "chan", None), check_vma=False
    )
```

profile of v0, /device:TPU:8, one launch (start us, length us, event | category | flops | bytes accessed | tf_op | source)
XLA Modules:
  0.0 518.0 jit_solution(13013517061511016048)
XLA Ops:
  6.5 0.0 all-gather.2.cloned.1.call-start
  6.5 1.6 fusion.81
  8.2 0.3 copy.36
  8.4 9.8 %collective-permute-start.1 = (f32[2,32,24,8]{1,3,2,0:T(8,128)S(1)}, f32[2,32,24,8]{1,3,2,0:T(8,128)S(1)}, u32[]{:S(2)}, u32[]{:S(2)}) collective-permute-start(f32[2,32,24,8]{1,3,2,0:T(8,128)S(1)} %copy.36), channel_id=1, source_target_pairs={{4,0},{8,4},{12,8},{16,12},{20,16},{24,20},{28,24},{32,28},{36,32}... | collective-permute-start | bytes 147464 | tf_op jit(solution)/shard_map/ppermute | solution.py:20
  18.3 0.3 copy.35
  18.5 0.1 collective-permute-start
  18.6 1.1 fusion.66
  19.6 1.0 fusion.67
  20.7 1.3 copy.22
  21.9 8.7 %collective-permute-done = f32[2,32,24,8]{1,3,2,0:T(8,128)S(1)} collective-permute-done((f32[2,32,24,8]{1,3,2,0:T(8,128)S(1)}, f32[2,32,24,8]{1,3,2,0:T(8,128)S(1)}, u32[]{:S(2)}, u32[]{:S(2)}) %collective-permute-start) | collective-permute-done | bytes 49184 | tf_op jit(solution)/shard_map/ppermute | solution.py:19
  30.6 0.3 copy.21
  30.9 0.0 collective-permute-done.1
  31.0 0.3 copy.26
  31.2 6.6 %fusion.14 = f32[2,32,24,128]{3,1,2,0:T(8,128)S(1)} fusion(f32[2,32,24,128]{3,1,2,0:T(8,128)S(1)} %copy.22, f32[2,32,24,8]{3,1,2,0:T(8,128)S(1)} %copy.26, f32[2,32,24,8]{3,1,2,0:T(8,128)S(1)} %copy.21, f32[24]{0:T(128)S(1)} %get-tuple-element.26, f32[24]{0:T(128)S(1)} %get-tuple-element.12, f32[24]{0:T(128)S(1)} %get-tuple-element.13, ...), kind=kLoop, calls=%fused_computation.39 | loop fusion | flops 9043968 | bytes 1672704 | tf_op jit(solution)/shard_map/add | solution.py:29
  37.8 0.1 fusion.64
  38.0 1.9 collective-permute-start.2
  39.9 3.6 collective-permute-start.3
  43.6 0.0 collective-permute-done.2
  43.6 1.6 collective-permute-done.3
  45.1 0.1 fusion.58
  45.2 0.9 divide_convert_fusion
  46.1 0.0 all-gather.2.cloned.1.call-update
  46.1 1.4 copy.27
  47.5 0.4 copy.29
  48.0 227.1 %all-gather.2.cloned.1.call-done = bf16[2,32,24,8192]{3,1,2,0:T(8,128)(2,1)} async-done(((bf16[2,32,24,128]{3,1,2,0:T(8,128)(2,1)}), bf16[2,32,24,8192]{3,1,2,0:T(8,128)(2,1)}) %all-gather.2.cloned.1.call-update) | async-done | bytes 25165840 | tf_op jit(solution)/shard_map/all_gather | solution.py:68
  275.1 0.0 slice-start
  275.1 0.0 slice-start.1
  275.1 0.0 slice-start.2
  275.1 0.0 slice-start.3
  275.1 0.0 slice-start.4
  275.1 0.0 slice-start.5
  275.1 46.2 %copy.28 = bf16[2,2,32,12,8192]{4,0,3,2,1:T(2,128)(2,1)} copy(bf16[2,2,32,12,8192]{4,2,3,0,1:T(8,128)(2,1)} %bitcast.52) | data formatting | bytes 50331648 | tf_op jit(solution)/shard_map/transpose | solution.py:44
  321.3 0.0 slice-done
  321.3 0.0 slice-done.1
  321.3 0.0 slice-done.2
  321.3 0.0 slice-done.3
  321.4 0.0 slice-done.4
  321.4 0.0 slice-done.5
  321.4 8.7 %slice_negate_fusion = (bf16[1,32,24,8192]{3,1,2,0:T(8,128)(2,1)}, bf16[1,32,24,8192]{3,1,2,0:T(8,128)(2,1)}) fusion(bf16[2,32,24,8192]{3,1,2,0:T(8,128)(2,1)S(1)} %bitcast.54), kind=kLoop, calls=%fused_computation.7 | loop fusion | flops 6291456 | bytes 50331648 | tf_op jit(solution)/shard_map/neg | solution.py:49
  330.1 11.8 %pad_maximum_fusion = bf16[2,32,24,8192]{3,1,2,0:T(8,128)(2,1)S(1)} fusion(bf16[1,32,24,8192]{3,1,2,0:T(8,128)(2,1)} %get-tuple-element.6, bf16[1,32,24,8192]{3,1,2,0:T(8,128)(2,1)} %get-tuple-element.5), kind=kLoop, calls=%fused_computation | loop fusion | flops 12582912 | bytes 50331648 | tf_op jit(solution)/shard_map/concatenate | solution.py:49
  341.9 53.3 %copy.31 = bf16[2,2,32,12,8192]{4,0,3,2,1:T(2,128)(2,1)} copy(bf16[2,2,32,12,8192]{4,2,3,0,1:T(8,128)(2,1)S(1)} %bitcast.57) | data formatting | bytes 50331648 | tf_op jit(solution)/shard_map/transpose | solution.py:44
  395.2 56.0 %fusion.5 = f32[2,1,128,8192]{3,2,0,1:T(8,128)S(1)} fusion(bf16[2,768,128]{1,2,0:T(8,128)(2,1)S(1)} %copy.29, bf16[2,768,8192]{2,0,1:T(2,128)(2,1)} %bitcast.55), kind=kOutput, calls=%fused_computation.8 | convolution fusion | flops 3221225472 | bytes 33947648 | tf_op jit(solution)/shard_map/bki,bkj->bij/dot_general | solution.py:71
  451.2 44.2 %fusion.8 = f32[2,1,128,8192]{3,2,0,1:T(8,128)} fusion(bf16[2,768,128]{1,2,0:T(8,128)(2,1)S(1)} %copy.29, bf16[2,768,8192]{2,0,1:T(2,128)(2,1)} %bitcast.56), kind=kOutput, calls=%fused_computation.9 | convolution fusion | flops 3221225472 | bytes 33947648 | tf_op jit(solution)/shard_map/bki,bkj->bij/dot_general | solution.py:72
  495.4 7.8 %fusion.4 = bf16[2,2,128,8192]{3,2,0,1:T(8,128)(2,1)} fusion(f32[2,1,128,8192]{3,2,0,1:T(8,128)} %fusion.8, f32[2,1,128,8192]{3,2,0,1:T(8,128)S(1)} %fusion.5), kind=kLoop, calls=%fused_computation.6 | loop fusion | flops 12582912 | bytes 25165824 | tf_op jit(solution)/shard_map/convert_element_type | solution.py:73
  503.2 7.8 %copy.34 = bf16[2,2,128,8192]{3,2,1,0:T(8,128)(2,1)} copy(bf16[2,2,128,8192]{3,2,0,1:T(8,128)(2,1)} %fusion.4) | data formatting | bytes 16777216 | tf_op jit(solution)/shard_map/convert_element_type | solution.py:73
  (2 shorter events, 0.0 us)
Async XLA Ops:
  6.5 268.6 %all-gather.2.cloned.1.call-start = ((), (), s32[]{:S(2)}) async-start(), calls=%async_computation | async-start | bytes 25559040 | tf_op jit(solution)/shard_map/all_gather | solution.py:68
  8.4 22.5 %collective-permute-start.1 = (f32[2,32,24,8]{1,3,2,0:T(8,128)S(1)}, f32[2,32,24,8]{1,3,2,0:T(8,128)S(1)}, u32[]{:S(2)}, u32[]{:S(2)}) collective-permute-start(f32[2,32,24,8]{1,3,2,0:T(8,128)S(1)} %copy.36), channel_id=1, source_target_pairs={{4,0},{8,4},{12,8},{16,12},{20,16},{24,20},{28,24},{32,28},{36,32}... | collective-permute-start | bytes 147464 | tf_op jit(solution)/shard_map/ppermute | solution.py:20
  18.5 12.1 %collective-permute-start = (f32[2,32,24,8]{1,3,2,0:T(8,128)S(1)}, f32[2,32,24,8]{1,3,2,0:T(8,128)S(1)}, u32[]{:S(2)}, u32[]{:S(2)}) collective-permute-start(f32[2,32,24,8]{1,3,2,0:T(8,128)S(1)} %copy.35), channel_id=1, source_target_pairs={{0,4},{4,8},{8,12},{12,16},{16,20},{20,24},{24,28},{28,32},{32,36}... | collective-permute-start | bytes 147464 | tf_op jit(solution)/shard_map/ppermute | solution.py:19
  38.0 5.6 %collective-permute-start.2 = (f32[32,2,128]{2,0,1:T(8,128)S(1)}, f32[32,2,128]{2,0,1:T(8,128)S(1)}, u32[]{:S(2)}, u32[]{:S(2)}) collective-permute-start(f32[32,2,128]{2,0,1:T(8,128)S(1)} %get-tuple-element.9), channel_id=1, source_target_pairs={{0,1},{1,2},{2,3},{4,5},{5,6},{6,7},{8,9},{9,10},{10,11},{12,13},{... | collective-permute-start | bytes 98312 | tf_op jit(solution)/shard_map/ppermute | solution.py:19
  39.9 5.2 %collective-permute-start.3 = (f32[32,2,128]{2,0,1:T(8,128)S(1)}, f32[32,2,128]{2,0,1:T(8,128)S(1)}, u32[]{:S(2)}, u32[]{:S(2)}) collective-permute-start(f32[32,2,128]{2,0,1:T(8,128)S(1)} %get-tuple-element.10), channel_id=1, source_target_pairs={{1,0},{2,1},{3,2},{5,4},{6,5},{7,6},{9,8},{10,9},{11,10},{13,12},{... | collective-permute-start | bytes 98312 | tf_op jit(solution)/shard_map/ppermute | solution.py:20
  275.1 46.2 %slice-start = ((s8[25165824]{0:T(1024)(128)(4,1)}), s8[4194304]{0:T(1024)(128)(4,1)S(1)}, s32[]{:S(2)}) async-start(s8[25165824]{0:T(1024)(128)(4,1)} %bitcast.53), calls=%async_computation.1 | async-start | bytes 8388608
  275.1 46.2 %slice-start.1 = ((s8[25165824]{0:T(1024)(128)(4,1)}), s8[4194304]{0:T(1024)(128)(4,1)S(1)}, s32[]{:S(2)}) async-start(s8[25165824]{0:T(1024)(128)(4,1)} %bitcast.53), calls=%async_computation.2 | async-start | bytes 8388608
  275.1 46.2 %slice-start.2 = ((s8[25165824]{0:T(1024)(128)(4,1)}), s8[4194304]{0:T(1024)(128)(4,1)S(1)}, s32[]{:S(2)}) async-start(s8[25165824]{0:T(1024)(128)(4,1)} %bitcast.53), calls=%async_computation.3 | async-start | bytes 8388608
  275.1 46.2 %slice-start.3 = ((s8[25165824]{0:T(1024)(128)(4,1)}), s8[4194304]{0:T(1024)(128)(4,1)S(1)}, s32[]{:S(2)}) async-start(s8[25165824]{0:T(1024)(128)(4,1)} %bitcast.53), calls=%async_computation.4 | async-start | bytes 8388608
  275.1 46.3 %slice-start.4 = ((s8[25165824]{0:T(1024)(128)(4,1)}), s8[4194304]{0:T(1024)(128)(4,1)S(1)}, s32[]{:S(2)}) async-start(s8[25165824]{0:T(1024)(128)(4,1)} %bitcast.53), calls=%async_computation.5 | async-start | bytes 8388608
  275.1 46.3 %slice-start.5 = ((s8[25165824]{0:T(1024)(128)(4,1)}), s8[4194304]{0:T(1024)(128)(4,1)S(1)}, s32[]{:S(2)}) async-start(s8[25165824]{0:T(1024)(128)(4,1)} %bitcast.53), calls=%async_computation.6 | async-start | bytes 8388608
Sparse Core Ops, SparseCore 0:
  46.3 228.7 all-gather.1
where the time goes:
time: 525 us; the launch traced here: 518 us
  waiting for transfers between devices  237 us (45%)
  local copies, waits for them, and re-layouts  115 us (22%)
  matrix products  100 us (19%)
  other arithmetic  35.9 us (7%)
  starting transfers between devices  15.4 us (3%)
  between operations  13.8 us (3%)
    all_gather x1, waiting for transfers between devices, body(): remote = lax.all_gather(whitened, 'chan', axis=3, tiled=True)  227 us
    transpose x3, local copies, waits for them, and re-layouts, arrange(): shaped = shaped.transpose(2, 0, 1, 3, 4)  101 us
    dot_general x1, matrix products, body(): jnp.einsum('bki,bkj->bij', features, right, preferred_element_type=jnp.fl...  56 us
    dot_general x1, matrix products, body(): jnp.einsum('bki,bkj->bij', features, turned, preferred_element_type=jnp.f...  44.2 us
    ppermute x2, starting transfers between devices, padded(): after = lax.ppermute(first, axis, down)  13.5 us
    concatenate x1, other arithmetic, partner(): return jnp.concatenate([-whitened[1:2], whitened[0:1]], axis=0)  11.8 us
  transfers between devices with their start and end apart: 5, of which 3 were waited for; matrix products, arithmetic and copies ran while one was open for 1% of the time, Pallas kernels for 0%

commit v1 on v0

--- a/solution.py
+++ b/solution.py
@@ -65,7 +65,9 @@
     band_count = local_bins // BAND_BINS
     features = arrange(whitened, band_count)
     scale_factor = 1.0 / (whitened.shape[1] * BAND_BINS)
-    remote = lax.all_gather(whitened, "chan", axis=3, tiled=True)
+    remote = jnp.concatenate(
+        lax.all_to_all(jnp.stack([whitened] * lax.axis_size("chan")), "chan", 0, 0), axis=3
+    )
     right = arrange(remote, band_count)
     turned = arrange(partner(remote), band_count)
     real_part = jnp.einsum("bki,bkj->bij", features, right, preferred_element_type=jnp.float32)

time: 525 us -> 1030 us (1.96)
  the two profiles are of different devices: /device:TPU:8 before, /device:TPU:101 now
where the time goes in v1:
time: 1030 us; the launch traced here: 1020 us
  waiting for transfers between devices  602 us (58%)
  local copies, waits for them, and re-layouts  250 us (24%)
  matrix products  100 us (10%)
  other arithmetic  43.8 us (4%)
  starting transfers between devices  28.8 us (3%)
    all_to_all x1, waiting for transfers between devices, body(): lax.all_to_all(jnp.stack([whitened] * lax.axis_size('chan')), 'chan', 0, 0)  598 us
    transpose x3, local copies, waits for them, and re-layouts, arrange(): shaped = shaped.transpose(2, 0, 1, 3, 4)  100 us
    dot_general x1, matrix products, body(): jnp.einsum('bki,bkj->bij', features, right, preferred_element_type=jnp.fl...  56 us
    dot_general x1, matrix products, body(): jnp.einsum('bki,bkj->bij', features, turned, preferred_element_type=jnp.f...  44.2 us
    another operation x1, local copies, waits for them, and re-layouts, arrange(): whitened.reshape(2, whitened.shape[1], band_count, BAND_BINS, whitened.sh...  37.3 us
    neg x2, local copies, waits for them, and re-layouts, partner(): return jnp.concatenate([-whitened[1:2], whitened[0:1]], axis=0)  28.5 us
    reshape x1, local copies, waits for them, and re-layouts, body(): jnp.concatenate(lax.all_to_all(jnp.stack([whitened] * lax.axis_size('chan...  26.8 us
  transfers between devices with their start and end apart: 5, of which 4 were waited for; matrix products, arithmetic and copies ran while one was open for 0% of the time, Pallas kernels for 0%

profile of v1, /device:TPU:101, one launch (start us, length us, event | category | flops | bytes accessed | tf_op | source)
XLA Modules:
  0.0 1024.6 jit_solution(16063989296478815750)
XLA Ops:
  0.0 1.7 fusion.81
  1.7 0.3 copy.37
  2.0 0.1 collective-permute-start.1
  2.0 0.3 copy.36
  2.3 2.9 collective-permute-start
  5.2 1.0 fusion.66
  6.2 1.0 fusion.67
  7.2 1.3 copy.20
  8.5 0.2 collective-permute-done
  8.7 0.3 copy.19
  8.9 0.4 collective-permute-done.1
  9.4 0.3 copy.24
  9.6 6.6 fusion.14
  16.2 0.1 fusion.64
  16.4 4.4 collective-permute-start.2
  20.8 1.9 collective-permute-start.3
  22.8 0.0 collective-permute-done.2
  22.8 3.3 collective-permute-done.3
  26.1 0.1 fusion.58
  26.1 0.1 divide_convert_fusion
  26.3 9.0 stack.8
  35.3 19.5 %all-to-all-start = ((bf16[64,2,32,24,128]{4,2,3,1,0:T(8,128)(2,1)}), bf16[64,2,32,24,128]{4,2,3,1,0:T(8,128)(2,1)}, u32[]{:S(2)}, u32[]{:S(2)}) async-start(bf16[64,2,32,24,128]{4,2,3,1,0:T(8,128)(2,1)} %stack.8), calls=%async_computation | async-start | bytes 50331648 | tf_op jit(solution)/shard_map/all_to_all | solution.py:69
  54.8 0.4 copy.25
  55.2 0.4 copy.28
  55.7 598.0 %all-to-all-done = bf16[64,2,32,24,128]{4,2,3,1,0:T(8,128)(2,1)} async-done(((bf16[64,2,32,24,128]{4,2,3,1,0:T(8,128)(2,1)}), bf16[64,2,32,24,128]{4,2,3,1,0:T(8,128)(2,1)}, u32[]{:S(2)}, u32[]{:S(2)}) %all-to-all-start) | async-done | bytes 25165856 | tf_op jit(solution)/shard_map/all_to_all | solution.py:69
  653.7 26.8 %copy.26 = bf16[2,32,24,64,128]{4,3,1,2,0:T(8,128)(2,1)} copy(bf16[2,32,24,64,128]{4,1,2,0,3:T(8,128)(2,1)} %bitcast.20) | data formatting | bytes 50331648 | tf_op jit(solution)/shard_map/reshape | solution.py:68
  680.5 17.4 %slice_negate_fusion = (bf16[1,32,24,64,128]{4,1,2,0,3:T(8,128)(2,1)}, bf16[1,32,24,64,128]{4,1,2,0,3:T(8,128)(2,1)}) fusion(bf16[2,32,24,64,128]{4,1,2,0,3:T(8,128)(2,1)} %bitcast.20), kind=kLoop, calls=%fused_computation.7 | loop fusion | flops 6291456 | bytes 50331648 | tf_op jit(solution)/shard_map/neg | solution.py:49
  697.9 37.3 %reshape_reshape.3 = bf16[2,32,2,12,8192]{4,1,3,2,0:T(8,128)(2,1)} reshape(bf16[2,32,24,64,128]{4,3,1,2,0:T(8,128)(2,1)} %copy.26) | data formatting | bytes 50331648 | tf_op jit(solution)/shard_map/reshape;reshape | solution.py:43
  735.2 0.0 copy-start
  735.2 46.2 %copy.27 = bf16[2,2,32,12,8192]{4,0,3,2,1:T(2,128)(2,1)} copy(bf16[2,2,32,12,8192]{4,2,3,0,1:T(8,128)(2,1)} %bitcast.64) | data formatting | bytes 50331648 | tf_op jit(solution)/shard_map/transpose | solution.py:44
  781.4 0.0 copy-done
  781.4 9.2 copy.30
  790.7 19.3 %neg.16 = bf16[1,32,2,12,8192]{4,1,3,2,0:T(8,128)(2,1)} reshape(bf16[1,32,24,64,128]{4,3,1,2,0:T(8,128)(2,1)} %copy.30) | data formatting | bytes 25165824 | tf_op jit(solution)/shard_map/neg | solution.py:49
  809.9 14.4 %copy.31 = bf16[1,32,24,64,128]{4,3,1,2,0:T(8,128)(2,1)} copy(bf16[1,32,24,64,128]{4,1,2,0,3:T(8,128)(2,1)} %get-tuple-element.6) | data formatting | bytes 25165824 | tf_op jit(solution)/shard_map/slice | solution.py:49
  824.4 19.3 %concatenate.39 = bf16[1,32,2,12,8192]{4,1,3,2,0:T(8,128)(2,1)} reshape(bf16[1,32,24,64,128]{4,3,1,2,0:T(8,128)(2,1)} %copy.31) | data formatting | bytes 25165824 | tf_op jit(solution)/shard_map/concatenate | solution.py:49
  843.7 11.8 %maximum_bitcast_fusion = bf16[2,2,32,12,8192]{4,2,3,0,1:T(8,128)(2,1)S(1)} fusion(bf16[1,32,2,12,8192]{4,1,3,2,0:T(8,128)(2,1)} %concatenate.39, bf16[1,32,2,12,8192]{4,1,3,2,0:T(8,128)(2,1)} %neg.16), kind=kLoop, calls=%fused_computation | loop fusion | flops 12582912 | bytes 50331648 | tf_op jit(solution)/shard_map/transpose | solution.py:44
  855.5 53.4 %copy.32 = bf16[2,2,32,12,8192]{4,0,3,2,1:T(2,128)(2,1)} copy(bf16[2,2,32,12,8192]{4,2,3,0,1:T(8,128)(2,1)S(1)} %maximum_bitcast_fusion) | data formatting | bytes 50331648 | tf_op jit(solution)/shard_map/transpose | solution.py:44
  908.8 56.0 %fusion.5 = f32[2,1,128,8192]{3,2,0,1:T(8,128)S(1)} fusion(bf16[2,768,128]{1,2,0:T(8,128)(2,1)S(1)} %copy.28, bf16[2,768,8192]{2,0,1:T(2,128)(2,1)} %bitcast.62), kind=kOutput, calls=%fused_computation.8 | convolution fusion | flops 3221225472 | bytes 33947648 | tf_op jit(solution)/shard_map/bki,bkj->bij/dot_general | solution.py:73
  964.8 44.2 %fusion.8 = f32[2,1,128,8192]{3,2,0,1:T(8,128)} fusion(bf16[2,768,128]{1,2,0:T(8,128)(2,1)S(1)} %copy.28, bf16[2,768,8192]{2,0,1:T(2,128)(2,1)} %bitcast.63), kind=kOutput, calls=%fused_computation.9 | convolution fusion | flops 3221225472 | bytes 33947648 | tf_op jit(solution)/shard_map/bki,bkj->bij/dot_general | solution.py:74
  1009.0 7.7 fusion.4
  1016.6 7.8 copy.35
  (1 shorter events, 0.0 us)
Async XLA Ops:
  2.0 7.4 collective-permute-start.1
  2.3 6.4 collective-permute-start
  16.4 6.4 collective-permute-start.2
  20.8 5.2 collective-permute-start.3
  35.3 618.4 %all-to-all-start = ((bf16[64,2,32,24,128]{4,2,3,1,0:T(8,128)(2,1)}), bf16[64,2,32,24,128]{4,2,3,1,0:T(8,128)(2,1)}, u32[]{:S(2)}, u32[]{:S(2)}) async-start(bf16[64,2,32,24,128]{4,2,3,1,0:T(8,128)(2,1)} %stack.8), calls=%async_computation | async-start | bytes 50331648 | tf_op jit(solution)/shard_map/all_to_all | solution.py:69
  735.2 46.2 %copy-start = (bf16[1,32,24,64,128]{4,1,2,0,3:T(8,128)(2,1)S(1)}, bf16[1,32,24,64,128]{4,1,2,0,3:T(8,128)(2,1)}, u32[]{:S(2)}) copy-start(bf16[1,32,24,64,128]{4,1,2,0,3:T(8,128)(2,1)} %get-tuple-element.5) | copy-start | bytes 37748740
